TPU v7x, 32 devices: a whole 2x2x4 slice. The times are simulated.
32 devices in a mesh: ctx: 16 (over z, y, core), fsdp: 2 (over x).
Axes of the slice: x: 2, y: 2, z: 4, core: 2. Of those that a mesh axis runs over, the one named last changes fastest.
Arguments:
- tokens: bfloat16 [2, 4096, 768], P('fsdp', 'ctx'), may hold values from -6 to 6
- lengths: int32 [2], P('fsdp'), may hold values from 1024 to 4096, as said below
- cotangent: bfloat16 [2, 4096, 768], P('fsdp', 'ctx'), may hold values from -6 to 6
- query_weight: bfloat16 [768, 768], P('ctx', 'fsdp'), may hold values from -0.21875 to 0.21875
- key_weight: bfloat16 [768, 768], P('ctx', 'fsdp'), may hold values from -0.21875 to 0.21875
- value_weight: bfloat16 [768, 768], P('ctx', 'fsdp'), may hold values from -0.21875 to 0.21875
- out_weight: bfloat16 [768, 768], P('ctx', 'fsdp'), may hold values from -6 to 6
- in_weight: bfloat16 [768, 3072], P('ctx', 'fsdp'), may hold values from -0.21875 to 0.21875
- down_weight: bfloat16 [3072, 768], P('ctx', 'fsdp'), may hold values from -0.109375 to 0.109375
- query_bias: bfloat16 [768], P('ctx'), may hold values from -3 to 3
- value_bias: bfloat16 [768], P('ctx'), may hold values from -0.119628906 to 0.119628906
- out_bias: bfloat16 [768], P('ctx'), may hold values from -3 to 3
- attn_norm_gain: bfloat16 [768], P('ctx'), may hold values from 0.5 to 1.5
- attn_norm_bias: bfloat16 [768], P('ctx'), may hold values from -2 to 2
- in_bias: bfloat16 [3072], P('ctx'), may hold values from -3 to 3
- down_bias: bfloat16 [768], P('ctx'), may hold values from -3 to 3
- ffn_norm_gain: bfloat16 [768], P('ctx'), may hold values from 0.5 to 1.5
- ffn_norm_bias: bfloat16 [768], P('ctx'), may hold values from -2 to 2
Outputs:
- layer_out: bfloat16 [2, 4096, 768], P('fsdp', 'ctx')
- tokens_grad: bfloat16 [2, 4096, 768], P('fsdp', 'ctx')
- grad_query_weight: float32 [768, 768], P('ctx', 'fsdp')
- grad_key_weight: float32 [768, 768], P('ctx', 'fsdp')
- grad_value_weight: float32 [768, 768], P('ctx', 'fsdp')
- grad_out_weight: float32 [768, 768], P('ctx', 'fsdp')
- grad_in_weight: float32 [768, 3072], P('ctx', 'fsdp')
- grad_down_weight: float32 [3072, 768], P('ctx', 'fsdp')
- grad_query_bias: float32 [768], P('ctx')
- grad_value_bias: float32 [768], P('ctx')
- grad_out_bias: float32 [768], P('ctx')
- grad_attn_norm_gain: float32 [768], P('ctx')
- grad_attn_norm_bias: float32 [768], P('ctx')
- grad_in_bias: float32 [3072], P('ctx')
- grad_down_bias: float32 [768], P('ctx')
- grad_ffn_norm_gain: float32 [768], P('ctx')
- grad_ffn_norm_bias: float32 [768], P('ctx')
- rms_values: float32 [3], replicated
Inputs may be any that keep to these rules, and one draw needn't show every extreme that they name: `lengths`: each sequence has between 1024 and 4096 valid slots; some sequence has exactly 4096, another exactly 1024.
All inputs are finite; a program needn't handle non-finite values.
Results may differ from a plain program's by a relative error of at most 0.022.
Values may be sent and summed in bfloat16 or wider, within the bound.
No kernel may reach another device: no remote copies, remote signals or barrier semaphores. Data moves between devices by JAX's collectives and lax.ppermute only.
A program may use at most 192 MiB of HBM per device.

v0:
```python
import jax
import jax.numpy as jnp
from jax import lax
from jax.sharding import PartitionSpec as P

HEAD_DIM = 64
norm_eps = 1e-12
score_scale = 0.125
masked_score = -1000000000.0
rows_contract = (((0,), (0,)), ((), ()))
columns_contract = (((1,), (1,)), ((), ()))


def layer_norm(stream, gain_vec, shift_vec):
    center = jnp.mean(stream, axis=-1, keepdims=True)
    offset = stream - center
    spread = jnp.mean(offset * offset, axis=-1, keepdims=True)
    return offset * lax.rsqrt(spread + norm_eps) * gain_vec + shift_vec


def gelu_exact(inner_pre):
    return jax.nn.gelu(inner_pre, approximate=False)


def plain_product(left_side, right_side):
    return jnp.dot(left_side, right_side, preferred_element_type=jnp.float32)


def row_product(left_side, right_side):
    return lax.dot_general(left_side, right_side, rows_contract, preferred_element_type=jnp.float32)


def column_product(left_side, right_side):
    return lax.dot_general(
        left_side, right_side, columns_contract, preferred_element_type=jnp.float32
    )


def head_scores(query_head, key_head, key_ok):
    scores = (
        jnp.einsum("sqd,skd->sqk", query_head, key_head, preferred_element_type=jnp.float32)
        * score_scale
    )
    return jnp.where(key_ok[:, None, :], scores, masked_score)


def attend(query_seq, pair_all, key_ok):
    seq_count, slot_count, model_width = query_seq.shape
    heads_count = model_width // HEAD_DIM

    def one_head(head_index, loop_state):
        mixed_out, log_totals = loop_state
        head_start = head_index * HEAD_DIM
        query_head = lax.dynamic_slice_in_dim(query_seq, head_start, HEAD_DIM, 2)
        key_head = lax.dynamic_slice_in_dim(pair_all, head_start, HEAD_DIM, 2)
        value_head = lax.dynamic_slice_in_dim(pair_all, model_width + head_start, HEAD_DIM, 2)
        scores = head_scores(query_head, key_head, key_ok)
        row_peak = jnp.max(scores, axis=-1, keepdims=True)
        row_expo = jnp.exp(scores - row_peak)
        row_total = jnp.sum(row_expo, axis=-1, keepdims=True)
        attn_probs = (row_expo / row_total).astype(jnp.bfloat16)
        head_out = jnp.einsum(
            "sqk,skd->sqd", attn_probs, value_head, preferred_element_type=jnp.float32
        )
        mixed_out = lax.dynamic_update_slice_in_dim(mixed_out, head_out, head_start, 2)
        log_row = row_peak[..., 0] + jnp.log(row_total[..., 0])
        log_totals = lax.dynamic_update_index_in_dim(log_totals, log_row, head_index, 0)
        return (mixed_out, log_totals)

    start_state = (
        jnp.zeros((seq_count, slot_count, model_width), jnp.float32),
        jnp.zeros((heads_count, seq_count, slot_count), jnp.float32),
    )
    return lax.fori_loop(0, heads_count, one_head, start_state)


def attend_back(query_seq, pair_all, key_ok, log_totals, grad_mixed):
    seq_count, slot_count, model_width = query_seq.shape
    heads_count = model_width // HEAD_DIM

    def one_head(head_index, loop_state):
        grad_query, grad_pair = loop_state
        head_start = head_index * HEAD_DIM
        query_head = lax.dynamic_slice_in_dim(query_seq, head_start, HEAD_DIM, 2)
        key_head = lax.dynamic_slice_in_dim(pair_all, head_start, HEAD_DIM, 2)
        value_head = lax.dynamic_slice_in_dim(pair_all, model_width + head_start, HEAD_DIM, 2)
        grad_head = lax.dynamic_slice_in_dim(grad_mixed, head_start, HEAD_DIM, 2)
        scores = head_scores(query_head, key_head, key_ok)
        log_row = lax.dynamic_index_in_dim(log_totals, head_index, 0, keepdims=False)
        attn_probs = jnp.exp(scores - log_row[..., None])
        probs_b = attn_probs.astype(jnp.bfloat16)
        grad_probs = jnp.einsum(
            "sqd,skd->sqk", grad_head, value_head, preferred_element_type=jnp.float32
        )
        row_inner = jnp.sum(attn_probs * grad_probs, axis=-1, keepdims=True)
        grad_scores = (attn_probs * (grad_probs - row_inner)).astype(jnp.bfloat16)
        grad_query_head = (
            jnp.einsum("sqk,skd->sqd", grad_scores, key_head, preferred_element_type=jnp.float32)
            * score_scale
        )
        grad_key_head = (
            jnp.einsum("sqk,sqd->skd", grad_scores, query_head, preferred_element_type=jnp.float32)
            * score_scale
        )
        grad_value_head = jnp.einsum(
            "sqk,sqd->skd", probs_b, grad_head, preferred_element_type=jnp.float32
        )
        grad_query = lax.dynamic_update_slice_in_dim(grad_query, grad_query_head, head_start, 2)
        grad_pair = lax.dynamic_update_slice_in_dim(grad_pair, grad_key_head, head_start, 2)
        grad_pair = lax.dynamic_update_slice_in_dim(
            grad_pair, grad_value_head, model_width + head_start, 2
        )
        return (grad_query, grad_pair)

    start_state = (jnp.zeros(query_seq.shape, jnp.float32), jnp.zeros(pair_all.shape, jnp.float32))
    return lax.fori_loop(0, heads_count, one_head, start_state)


def column_sums(matrix_b):
    return jnp.sum(matrix_b.astype(jnp.float32), axis=0)


def body(
    tokens,
    lengths,
    cotangent,
    query_weight,
    key_weight,
    value_weight,
    out_weight,
    in_weight,
    down_weight,
    query_bias,
    value_bias,
    out_bias,
    attn_norm_gain,
    attn_norm_bias,
    in_bias,
    down_bias,
    ffn_norm_gain,
    ffn_norm_bias,
):
    seq_count, slot_count, model_width = tokens.shape
    row_count = seq_count * slot_count
    ctx_size = lax.axis_size("ctx")
    ctx_index = lax.axis_index("ctx")
    row_parts = (
        lax.all_gather(query_weight, "ctx", axis=0, tiled=True),
        lax.all_gather(key_weight, "ctx", axis=0, tiled=True),
        lax.all_gather(value_weight, "ctx", axis=0, tiled=True),
        lax.all_gather(out_weight, "ctx", axis=0, tiled=True),
        lax.all_gather(in_weight, "ctx", axis=0, tiled=True),
        lax.all_gather(down_weight, "ctx", axis=0, tiled=True),
        lax.all_gather(query_bias, "ctx", axis=0, tiled=True),
        lax.all_gather(value_bias, "ctx", axis=0, tiled=True),
        lax.all_gather(out_bias, "ctx", axis=0, tiled=True),
        lax.all_gather(attn_norm_gain, "ctx", axis=0, tiled=True),
        lax.all_gather(attn_norm_bias, "ctx", axis=0, tiled=True),
        lax.all_gather(in_bias, "ctx", axis=0, tiled=True),
        lax.all_gather(down_bias, "ctx", axis=0, tiled=True),
        lax.all_gather(ffn_norm_gain, "ctx", axis=0, tiled=True),
        lax.all_gather(ffn_norm_bias, "ctx", axis=0, tiled=True),
    )
    full_mats = (
        lax.all_gather(row_parts[0], "fsdp", axis=1, tiled=True),
        lax.all_gather(row_parts[1], "fsdp", axis=1, tiled=True),
        lax.all_gather(row_parts[2], "fsdp", axis=1, tiled=True),
        lax.all_gather(row_parts[3], "fsdp", axis=1, tiled=True),
        lax.all_gather(row_parts[4], "fsdp", axis=1, tiled=True),
        lax.all_gather(row_parts[5], "fsdp", axis=1, tiled=True),
    )
    query_full, key_full, value_full, out_full, in_full, down_full = full_mats
    query_vec = row_parts[6].astype(jnp.float32)
    value_vec = row_parts[7].astype(jnp.float32)
    out_vec = row_parts[8].astype(jnp.float32)
    gain_one = row_parts[9].astype(jnp.float32)
    bias_one = row_parts[10].astype(jnp.float32)
    in_vec = row_parts[11].astype(jnp.float32)
    down_vec = row_parts[12].astype(jnp.float32)
    gain_two = row_parts[13].astype(jnp.float32)
    bias_two = row_parts[14].astype(jnp.float32)
    local_slots = ctx_index * slot_count + jnp.arange(slot_count)
    local_ok = local_slots[None, :] < lengths[:, None]
    valid_mask = local_ok.astype(jnp.float32)
    valid_col = valid_mask.reshape(row_count, 1)
    key_ok = jnp.arange(slot_count * ctx_size)[None, :] < lengths[:, None]
    token_rows = tokens.reshape(row_count, model_width)
    queries_b = (plain_product(token_rows, query_full) + query_vec).astype(jnp.bfloat16)
    keys_b = plain_product(token_rows, key_full).astype(jnp.bfloat16)
    values_b = (plain_product(token_rows, value_full) + value_vec).astype(jnp.bfloat16)
    pair_local = jnp.concatenate([keys_b, values_b], axis=1).reshape(
        seq_count, slot_count, 2 * model_width
    )
    pair_all = lax.all_gather(pair_local, "ctx", axis=1, tiled=True)
    query_seq = queries_b.reshape(seq_count, slot_count, model_width)
    mixed_out, log_totals = attend(query_seq, pair_all, key_ok)
    mixed_b = mixed_out.reshape(row_count, model_width).astype(jnp.bfloat16)
    attn_branch = plain_product(mixed_b, out_full) + out_vec
    stream = token_rows.astype(jnp.float32) + attn_branch
    norm_one, norm_one_back = jax.vjp(layer_norm, stream, gain_one, bias_one)
    norm_one_b = norm_one.astype(jnp.bfloat16)
    inner_pre = plain_product(norm_one_b, in_full) + in_vec
    act_out, gelu_back = jax.vjp(gelu_exact, inner_pre)
    act_b = act_out.astype(jnp.bfloat16)
    ffn_branch = plain_product(act_b, down_full) + down_vec
    stream_two = norm_one + ffn_branch
    final_out, norm_two_back = jax.vjp(layer_norm, stream_two, gain_two, bias_two)
    layer_out = (
        (valid_col * final_out).astype(jnp.bfloat16).reshape(seq_count, slot_count, model_width)
    )
    grad_final = valid_col * cotangent.reshape(row_count, model_width).astype(jnp.float32)
    grad_stream_two, grad_gain_two, grad_bias_two = norm_two_back(grad_final)
    grad_ffn_b = grad_stream_two.astype(jnp.bfloat16)
    grad_down_vec = column_sums(grad_ffn_b)
    grad_down_full = row_product(act_b, grad_ffn_b)
    grad_inner_b = gelu_back(column_product(grad_ffn_b, down_full))[0].astype(jnp.bfloat16)
    grad_in_vec = column_sums(grad_inner_b)
    grad_in_full = row_product(norm_one_b, grad_inner_b)
    grad_norm_one = grad_stream_two + column_product(grad_inner_b, in_full)
    grad_stream, grad_gain_one, grad_bias_one = norm_one_back(grad_norm_one)
    grad_attn_b = grad_stream.astype(jnp.bfloat16)
    grad_out_vec = column_sums(grad_attn_b)
    grad_out_full = row_product(mixed_b, grad_attn_b)
    grad_mixed = (
        column_product(grad_attn_b, out_full)
        .astype(jnp.bfloat16)
        .reshape(seq_count, slot_count, model_width)
    )
    grad_query_seq, grad_pair = attend_back(query_seq, pair_all, key_ok, log_totals, grad_mixed)
    grad_pair_local = lax.psum_scatter(
        grad_pair.astype(jnp.bfloat16), "ctx", scatter_dimension=1, tiled=True
    ).astype(jnp.float32)
    grad_keys_b = (
        grad_pair_local[:, :, :model_width].reshape(row_count, model_width).astype(jnp.bfloat16)
    )
    grad_values_b = (
        grad_pair_local[:, :, model_width:].reshape(row_count, model_width).astype(jnp.bfloat16)
    )
    grad_queries_b = grad_query_seq.reshape(row_count, model_width).astype(jnp.bfloat16)
    grad_query_full = row_product(token_rows, grad_queries_b)
    grad_query_vec = column_sums(grad_queries_b)
    grad_key_full = row_product(token_rows, grad_keys_b)
    grad_value_full = row_product(token_rows, grad_values_b)
    grad_value_vec = column_sums(grad_values_b)
    tokens_grad = (
        (
            grad_stream
            + column_product(grad_queries_b, query_full)
            + column_product(grad_keys_b, key_full)
            + column_product(grad_values_b, value_full)
        )
        .astype(jnp.bfloat16)
        .reshape(seq_count, slot_count, model_width)
    )
    narrow = (
        lax.psum_scatter(
            grad_query_full.astype(jnp.bfloat16), "fsdp", scatter_dimension=1, tiled=True
        ).astype(jnp.float32),
        lax.psum_scatter(
            grad_key_full.astype(jnp.bfloat16), "fsdp", scatter_dimension=1, tiled=True
        ).astype(jnp.float32),
        lax.psum_scatter(
            grad_value_full.astype(jnp.bfloat16), "fsdp", scatter_dimension=1, tiled=True
        ).astype(jnp.float32),
        lax.psum_scatter(
            grad_out_full.astype(jnp.bfloat16), "fsdp", scatter_dimension=1, tiled=True
        ).astype(jnp.float32),
        lax.psum_scatter(
            grad_in_full.astype(jnp.bfloat16), "fsdp", scatter_dimension=1, tiled=True
        ).astype(jnp.float32),
        lax.psum_scatter(
            grad_down_full.astype(jnp.bfloat16), "fsdp", scatter_dimension=1, tiled=True
        ).astype(jnp.float32),
    )
    owned_grads = (
        lax.psum_scatter(
            narrow[0].astype(jnp.bfloat16), "ctx", scatter_dimension=0, tiled=True
        ).astype(jnp.float32),
        lax.psum_scatter(
            narrow[1].astype(jnp.bfloat16), "ctx", scatter_dimension=0, tiled=True
        ).astype(jnp.float32),
        lax.psum_scatter(
            narrow[2].astype(jnp.bfloat16), "ctx", scatter_dimension=0, tiled=True
        ).astype(jnp.float32),
        lax.psum_scatter(
            narrow[3].astype(jnp.bfloat16), "ctx", scatter_dimension=0, tiled=True
        ).astype(jnp.float32),
        lax.psum_scatter(
            narrow[4].astype(jnp.bfloat16), "ctx", scatter_dimension=0, tiled=True
        ).astype(jnp.float32),
        lax.psum_scatter(
            narrow[5].astype(jnp.bfloat16), "ctx", scatter_dimension=0, tiled=True
        ).astype(jnp.float32),
    )
    moments = jnp.stack(
        [
            jnp.sum(valid_col * stream * stream),
            jnp.sum(valid_col * attn_branch * attn_branch),
            jnp.sum(valid_col * ffn_branch * ffn_branch),
            jnp.sum(valid_col),
        ]
    )
    summed = lax.psum(
        (
            moments,
            grad_query_vec,
            grad_value_vec,
            grad_out_vec,
            grad_gain_one,
            grad_bias_one,
            grad_in_vec,
            grad_down_vec,
            grad_gain_two,
            grad_bias_two,
        ),
        ("ctx", "fsdp"),
    )
    width_shard = query_bias.shape[0]
    hidden_shard = in_bias.shape[0]

    def own_piece(vector_full, shard_len):
        return lax.dynamic_slice_in_dim(vector_full, ctx_index * shard_len, shard_len, 0)

    rms_values = jnp.sqrt(summed[0][:3] / (summed[0][3] * model_width))
    return (
        layer_out,
        tokens_grad,
        owned_grads[0],
        owned_grads[1],
        owned_grads[2],
        owned_grads[3],
        owned_grads[4],
        owned_grads[5],
        own_piece(summed[1], width_shard),
        own_piece(summed[2], width_shard),
        own_piece(summed[3], width_shard),
        own_piece(summed[4], width_shard),
        own_piece(summed[5], width_shard),
        own_piece(summed[6], hidden_shard),
        own_piece(summed[7], width_shard),
        own_piece(summed[8], width_shard),
        own_piece(summed[9], width_shard),
        rms_values,
    )


def solution(mesh):
    in_specs = (
        P("fsdp", "ctx", None),
        P("fsdp"),
        P("fsdp", "ctx", None),
        P("ctx", "fsdp"),
        P("ctx", "fsdp"),
        P("ctx", "fsdp"),
        P("ctx", "fsdp"),
        P("ctx", "fsdp"),
        P("ctx", "fsdp"),
        P("ctx"),
        P("ctx"),
        P("ctx"),
        P("ctx"),
        P("ctx"),
        P("ctx"),
        P("ctx"),
        P("ctx"),
        P("ctx"),
    )
    out_specs = (
        P("fsdp", "ctx", None),
        P("fsdp", "ctx", None),
        P("ctx", "fsdp"),
        P("ctx", "fsdp"),
        P("ctx", "fsdp"),
        P("ctx", "fsdp"),
        P("ctx", "fsdp"),
        P("ctx", "fsdp"),
        P("ctx"),
        P("ctx"),
        P("ctx"),
        P("ctx"),
        P("ctx"),
        P("ctx"),
        P("ctx"),
        P("ctx"),
        P("ctx"),
        P(),
    )
    return jax.shard_map(body, mesh=mesh, in_specs=in_specs, out_specs=out_specs, check_vma=False)
```

profile of v0, /device:TPU:0, one launch (start us, length us, event | category | flops | bytes accessed | tf_op | source)
XLA Modules:
  0.0 1333.6 jit_solution(6212013291559108767)
XLA Ops:
  7.4 26.6 %all_gather.69 = bf16[768,384]{1,0:T(8,128)(2,1)} all-gather(bf16[48,384]{1,0:T(8,128)(2,1)} %param.26), channel_id=1, replica_groups=mesh['ctx'=16,'fsdp'=2] {'ctx'}, dimensions={0}, use_global_device_ids=true | all-gather | bytes 626688 | tf_op jit(solution)/shard_map/all_gather | solution.py:149
  34.1 20.7 %all_gather.71 = bf16[768,384]{1,0:T(8,128)(2,1)} all-gather(bf16[48,384]{1,0:T(8,128)(2,1)} %param.27), channel_id=1, replica_groups=mesh['ctx'=16,'fsdp'=2] {'ctx'}, dimensions={0}, use_global_device_ids=true | all-gather | bytes 626688 | tf_op jit(solution)/shard_map/all_gather | solution.py:150
  55.6 22.2 %all_gather.66 = bf16[768,384]{1,0:T(8,128)(2,1)} all-gather(bf16[48,384]{1,0:T(8,128)(2,1)} %param.25), channel_id=1, replica_groups=mesh['ctx'=16,'fsdp'=2] {'ctx'}, dimensions={0}, use_global_device_ids=true | all-gather | bytes 626688 | tf_op jit(solution)/shard_map/all_gather | solution.py:148
  82.5 58.1 %all-reduce.10 = (bf16[768]{0:T(1024)(128)(2,1)S(1)}, bf16[768]{0:T(1024)(128)(2,1)S(1)}, bf16[3072]{0:T(1024)(128)(2,1)S(1)}, bf16[768]{0:T(1024)(128)(2,1)S(1)...) all-reduce(bf16[768]{0:T(1024)(128)(2,1)S(1)} %dynamic-update-slice, ...), channel_id=1, replica_groups=mesh['ctx'=16,'fsdp'=2] {'ctx'}, use_global_device_ids=true, to_apply=%add | all-reduce | flops 9216 | bytes 36864
  145.2 20.6 %all_gather.75 = bf16[768,384]{1,0:T(8,128)(2,1)} all-gather(bf16[48,384]{1,0:T(8,128)(2,1)S(1)} %copy-done.13), channel_id=1, replica_groups=mesh['ctx'=16,'fsdp'=2] {'ctx'}, dimensions={0}, use_global_device_ids=true | all-gather | bytes 626688 | tf_op jit(solution)/shard_map/all_gather | solution.py:151
  169.1 21.9 %all-gather.23.cloned.1.call-done = bf16[3072,384]{1,0:T(8,128)(2,1)} async-done(((bf16[192,384]{1,0:T(8,128)(2,1)}), bf16[3072,384]{1,0:T(8,128)(2,1)}) %all-gather.23.cloned.1.call-update) | async-done | bytes 2359312 | tf_op jit(solution)/shard_map/all_gather | solution.py:153
  191.4 101.4 %all-gather.27.cloned.1.call-done = bf16[4096,1536]{1,0:T(8,128)(2,1)} async-done(((bf16[256,1536]{1,0:T(8,128)(2,1)}), bf16[4096,1536]{1,0:T(8,128)(2,1)}) %all-gather.27.cloned.1.call-update) | async-done | bytes 12582928 | tf_op jit(solution)/shard_map/all_gather | solution.py:194
  292.8 77.5 %while.36 = (s32[]{:T(128)}, bf16[1,256,768]{1,2,0:T(8,128)(2,1)S(1)}, f32[12,1,256]{2,1,0:T(1,128)S(1)}, bf16[1,256,768]{2,1,0:T(8,128)(2,1)S(1)}, bf16[1,4096,...) while((s32[]{:T(128)}, ...), condition=%wide.region_3.4_spmd.clone, body=%wide.region_0.3_spmd.clone.sunk | while | flops 276827904 | bytes 14829822 | solution.py:74
  322.3 2.9 fusion.147
  328.9 2.8 fusion.147
  372.6 6.9 all-gather.21.cloned.1.call-done
  379.5 12.1 multiply_convert_fusion.1
  391.6 52.1 %all-gather.25.cloned.1.call-done = bf16[3072,768]{1,0:T(8,128)(2,1)} async-done(((bf16[3072,384]{1,0:T(8,128)(2,1)}), bf16[3072,768]{1,0:T(8,128)(2,1)}) %all-gather.25.cloned.1.call-update) | async-done | bytes 4718608 | tf_op jit(solution)/shard_map/all_gather | solution.py:170
  443.8 4.4 fusion.101
  451.8 2.7 convert_reduce_fusion
  458.8 6.1 broadcast_in_dim.102
  464.8 142.2 %while.37 = (s32[]{:T(128)}, bf16[1,256,768]{1,2,0:T(8,128)(2,1)S(1)}, bf16[1,4096,1536]{1,2,0:T(8,128)(2,1)}, bf16[1,256,768]{2,1,0:T(8,128)(2,1)S(1)}, bf16[1,...) while((s32[]{:T(128)}, ...), condition=%wide.region_14.15_spmd.clone, body=%wide.region_12.14_spmd.clone.sunk | while | flops 680808192 | bytes 37041444 | solution.py:116
  467.8 2.8 multiply_reduce_fusion.6
  479.6 2.7 multiply_reduce_fusion.6
  491.5 2.8 multiply_reduce_fusion.6
  503.3 2.8 multiply_reduce_fusion.6
  515.1 2.7 multiply_reduce_fusion.6
  526.9 2.7 multiply_reduce_fusion.6
  538.8 2.7 multiply_reduce_fusion.6
  550.6 2.7 multiply_reduce_fusion.6
  562.5 2.8 multiply_reduce_fusion.6
  574.3 2.8 multiply_reduce_fusion.6
  586.1 2.8 multiply_reduce_fusion.6
  598.0 2.8 multiply_reduce_fusion.6
  611.9 5.7 convolution_convert_fusion.1
  619.4 3.7 convolution_convert_fusion
  623.1 7.1 copy.50
  630.3 111.7 %reduce-scatter.24.cloned.1.call-done = bf16[1,256,1536]{1,2,0:T(8,128)(2,1)} async-done(((bf16[1,4096,1536]{1,2,0:T(8,128)(2,1)}), bf16[1,256,1536]{1,2,0:T(8,128)(2,1)}) %reduce-scatter.24.cloned.1.call-update) | async-done | bytes 786448 | tf_op jit(solution)/shard_map/reduce_scatter | solution.py:230
  744.6 20.6 %reduce-scatter.26.cloned.1.call-done = bf16[768,384]{0,1:T(8,128)(2,1)} async-done(((bf16[768,768]{0,1:T(8,128)(2,1)}), bf16[768,384]{0,1:T(8,128)(2,1)}) %reduce-scatter.26.cloned.1.call-update) | async-done | bytes 589840 | tf_op jit(solution)/shard_map/reduce_scatter | solution.py:256
  767.4 21.8 %reduce-scatter.46.cloned.1.call-done = bf16[384,768]{1,0:T(8,128)(2,1)} async-done(((bf16[768,768]{1,0:T(8,128)(2,1)}), bf16[384,768]{1,0:T(8,128)(2,1)}) %reduce-scatter.46.cloned.1.call-update) | async-done | bytes 589840
  791.4 60.1 %reduce-scatter.34.cloned.1.call-done = bf16[768,1536]{1,0:T(8,128)(2,1)} async-done(((bf16[768,3072]{1,0:T(8,128)(2,1)}), bf16[768,1536]{1,0:T(8,128)(2,1)}) %reduce-scatter.34.cloned.1.call-update) | async-done | bytes 2359312 | tf_op jit(solution)/shard_map/reduce_scatter | solution.py:268
  851.5 62.2 %reduce-scatter.48.cloned.1.call-done = bf16[384,3072]{1,0:T(8,128)(2,1)} async-done(((bf16[768,3072]{1,0:T(8,128)(2,1)}), bf16[384,3072]{1,0:T(8,128)(2,1)}) %reduce-scatter.48.cloned.1.call-update) | async-done | bytes 2359312
  913.8 4.4 copy.51
  919.8 17.8 %reduce-scatter.28.cloned.1.call-done = bf16[768,384]{0,1:T(8,128)(2,1)} async-done(((bf16[768,768]{0,1:T(8,128)(2,1)}), bf16[768,384]{0,1:T(8,128)(2,1)}) %reduce-scatter.28.cloned.1.call-update) | async-done | bytes 589840 | tf_op jit(solution)/shard_map/reduce_scatter | solution.py:259
  943.6 2.8 convolution_add_fusion.3
  946.4 49.9 %reduce-scatter.40.cloned.1.call-done = bf16[48,384]{1,0:T(8,128)(2,1)} async-done(((bf16[768,384]{1,0:T(8,128)(2,1)}), bf16[48,384]{1,0:T(8,128)(2,1)}) %reduce-scatter.40.cloned.1.call-update) | async-done | bytes 36880
  998.0 55.7 %reduce-scatter.32.cloned.1.call-done = bf16[48,384]{1,0:T(8,128)(2,1)} async-done(((bf16[768,384]{1,0:T(8,128)(2,1)}), bf16[48,384]{1,0:T(8,128)(2,1)}) %reduce-scatter.32.cloned.1.call-update) | async-done | bytes 36880 | tf_op jit(solution)/shard_map/reduce_scatter | solution.py:285
  1055.0 64.8 %reduce-scatter.36.cloned.1.call-done = bf16[48,1536]{1,0:T(8,128)(2,1)} async-done(((bf16[768,1536]{1,0:T(8,128)(2,1)}), bf16[48,1536]{1,0:T(8,128)(2,1)}) %reduce-scatter.36.cloned.1.call-update) | async-done | bytes 147472 | tf_op jit(solution)/shard_map/reduce_scatter | solution.py:288
  1121.5 64.1 %reduce-scatter.38.cloned.1.call-done = bf16[192,384]{1,0:T(8,128)(2,1)} async-done(((bf16[3072,384]{1,0:T(8,128)(2,1)}), bf16[192,384]{1,0:T(8,128)(2,1)}) %reduce-scatter.38.cloned.1.call-update) | async-done | bytes 147472 | tf_op jit(solution)/shard_map/reduce_scatter | solution.py:291
  1187.2 21.3 %reduce-scatter.30.cloned.1.call-done = bf16[768,384]{0,1:T(8,128)(2,1)} async-done(((bf16[768,768]{0,1:T(8,128)(2,1)}), bf16[768,384]{0,1:T(8,128)(2,1)}) %reduce-scatter.30.cloned.1.call-update) | async-done | bytes 589840 | tf_op jit(solution)/shard_map/reduce_scatter | solution.py:262
  1210.9 40.5 %all-reduce.9 = (f32[768]{0:T(1024)S(1)}, f32[768]{0:T(1024)S(1)}, f32[768]{0:T(1024)S(1)}, f32[768]{0:T(1024)S(1)}, f32[768]{0:T(1024)S(1)}, /*index=5*/f32[307...) all-reduce(f32[768]{0:T(1024)S(1)} %convert_reduce_fusion.4, ...), channel_id=1, replica_groups=mesh['ctx'=16,'fsdp'=2] {'ctx','fsdp'}, use_global_device_ids=true, to_apply=%region_29.30 | all-reduce | flops 9220 | bytes 73760 | tf_op jit(solution)/shard_map/psum | solution.py:303
  1260.3 6.8 reduce-scatter.42.cloned.1.call-done
  1268.7 56.3 %reduce-scatter.44.cloned.1.call-done = bf16[48,384]{1,0:T(8,128)(2,1)} async-done(((bf16[768,384]{1,0:T(8,128)(2,1)}), bf16[48,384]{1,0:T(8,128)(2,1)}) %reduce-scatter.44.cloned.1.call-update) | async-done | bytes 36880
  (367 shorter events, 242.9 us)
Async XLA Ops:
  7.2 71.3 %copy-start.32 = (u32[32]{0:T(128)S(1)}, u32[32]{0:T(128)}, u32[]{:S(2)}) copy-start(u32[32]{0:T(128)} %constant.307) | copy-start | bytes 388
  7.2 73.1 %copy-start.23 = (bf16[48]{0:T(256)(128)(2,1)S(1)}, bf16[48]{0:T(256)(128)(2,1)}, u32[]{:S(2)}) copy-start(bf16[48]{0:T(256)(128)(2,1)} %param.38) | copy-start | bytes 292
  7.2 73.4 %copy-start.24 = (bf16[48]{0:T(256)(128)(2,1)S(1)}, bf16[48]{0:T(256)(128)(2,1)}, u32[]{:S(2)}) copy-start(bf16[48]{0:T(256)(128)(2,1)} %param.37) | copy-start | bytes 292
  7.2 73.6 %copy-start.25 = (bf16[48]{0:T(256)(128)(2,1)S(1)}, bf16[48]{0:T(256)(128)(2,1)}, u32[]{:S(2)}) copy-start(bf16[48]{0:T(256)(128)(2,1)} %param.34) | copy-start | bytes 292
  7.2 73.8 %copy-start.26 = (bf16[48]{0:T(256)(128)(2,1)S(1)}, bf16[48]{0:T(256)(128)(2,1)}, u32[]{:S(2)}) copy-start(bf16[48]{0:T(256)(128)(2,1)} %param.35) | copy-start | bytes 292
  7.2 74.1 %copy-start.27 = (bf16[48]{0:T(256)(128)(2,1)S(1)}, bf16[48]{0:T(256)(128)(2,1)}, u32[]{:S(2)}) copy-start(bf16[48]{0:T(256)(128)(2,1)} %param.33) | copy-start | bytes 292
  7.3 74.3 %copy-start.28 = (bf16[48]{0:T(256)(128)(2,1)S(1)}, bf16[48]{0:T(256)(128)(2,1)}, u32[]{:S(2)}) copy-start(bf16[48]{0:T(256)(128)(2,1)} %param.32) | copy-start | bytes 292
  7.3 74.5 %copy-start.29 = (bf16[48]{0:T(256)(128)(2,1)S(1)}, bf16[48]{0:T(256)(128)(2,1)}, u32[]{:S(2)}) copy-start(bf16[48]{0:T(256)(128)(2,1)} %param.31) | copy-start | bytes 292
  7.3 74.7 %copy-start.30 = (bf16[48]{0:T(256)(128)(2,1)S(1)}, bf16[48]{0:T(256)(128)(2,1)}, u32[]{:S(2)}) copy-start(bf16[48]{0:T(256)(128)(2,1)} %param.39) | copy-start | bytes 292
  7.3 75.0 %copy-start.31 = (bf16[192]{0:T(256)(128)(2,1)S(1)}, bf16[192]{0:T(256)(128)(2,1)}, u32[]{:S(2)}) copy-start(bf16[192]{0:T(256)(128)(2,1)} %param.36) | copy-start | bytes 1156
  7.3 133.3 %copy-start = (bf16[1,256,768]{2,1,0:T(8,128)(2,1)S(1)}, bf16[1,256,768]{2,1,0:T(8,128)(2,1)}, u32[]{:S(2)}) copy-start(bf16[1,256,768]{2,1,0:T(8,128)(2,1)} %param.22) | copy-start | bytes 1179652
  7.3 133.3 %all-gather.13.cloned.1.call-start = ((), (), s32[]{:S(2)}) async-start(), calls=%async_computation.14 | async-start | bytes 1769472 | tf_op jit(solution)/shard_map/all_gather | solution.py:166
  34.0 108.4 %all-gather.15.cloned.1.call-start = ((), (), s32[]{:S(2)}) async-start(), calls=%async_computation.15 | async-start | bytes 1769472 | tf_op jit(solution)/shard_map/all_gather | solution.py:167
  54.8 111.1 %all-gather.19.cloned.1.call-start = ((), (), s32[]{:S(2)}) async-start(), calls=%async_computation.17 | async-start | bytes 2506752 | tf_op jit(solution)/shard_map/all_gather | solution.py:152
  55.5 111.9 %all-gather.11.cloned.1.call-start = ((), (), s32[]{:S(2)}) async-start(), calls=%async_computation.13 | async-start | bytes 1769472 | tf_op jit(solution)/shard_map/all_gather | solution.py:165
  77.8 113.3 %all-gather.23.cloned.1.call-start = ((), (), s32[]{:S(2)}) async-start(), calls=%async_computation.19 | async-start | bytes 2506752 | tf_op jit(solution)/shard_map/all_gather | solution.py:153
  78.4 214.4 %all-gather.27.cloned.1.call-start = ((), (), s32[]{:S(2)}) async-start(), calls=%async_computation.29 | async-start | bytes 13369344 | tf_op jit(solution)/shard_map/all_gather | solution.py:194
  140.6 4.6 copy-start.13
  145.1 225.2 %all-gather.17.cloned.1.call-start = ((), (), s32[]{:S(2)}) async-start(), calls=%async_computation.16 | async-start | bytes 1769472 | tf_op jit(solution)/shard_map/all_gather | solution.py:168
  165.8 213.7 %all-gather.21.cloned.1.call-start = ((), (), s32[]{:S(2)}) async-start(), calls=%async_computation.18 | async-start | bytes 7077888 | tf_op jit(solution)/shard_map/all_gather | solution.py:169
  166.5 277.2 %all-gather.25.cloned.1.call-start = ((), (), s32[]{:S(2)}) async-start(), calls=%async_computation.20 | async-start | bytes 7077888 | tf_op jit(solution)/shard_map/all_gather | solution.py:170
  191.1 550.9 %reduce-scatter.24.cloned.1.call-start = ((), (), s32[]{:S(2)}) async-start(), calls=%async_computation.21 | async-start | bytes 13369344 | tf_op jit(solution)/shard_map/reduce_scatter | solution.py:230
  370.3 21.3 %copy-start.4 = (bf16[1,256,768]{1,2,0:T(8,128)(2,1)}, bf16[1,256,768]{1,2,0:T(8,128)(2,1)S(1)}, u32[]{:S(2)}) copy-start(bf16[1,256,768]{1,2,0:T(8,128)(2,1)S(1)} %get-tuple-element.372) | copy-start | bytes 1179652
  372.6 84.3 %copy-start.17 = (f32[256]{0:T(256)}, f32[256]{0:T(256)S(1)}, u32[]{:S(2)}) copy-start(f32[256]{0:T(256)S(1)} %fusion.90) | copy-start | bytes 3076
  443.8 4.7 copy-start.10
  443.8 8.0 copy-start.33
  443.8 8.0 copy-start.34
  607.1 158.1 %reduce-scatter.26.cloned.1.call-start = ((), (), s32[]{:S(2)}) async-start(), calls=%async_computation.22 | async-start | bytes 1769472 | tf_op jit(solution)/shard_map/reduce_scatter | solution.py:256
  608.7 180.4 %reduce-scatter.46.cloned.1.call-start = ((), (), s32[]{:S(2)}) async-start(), calls=%async_computation.33 | async-start | bytes 1769472
  611.8 239.6 %reduce-scatter.34.cloned.1.call-start = ((), (), s32[]{:S(2)}) async-start(), calls=%async_computation.26 | async-start | bytes 7077888 | tf_op jit(solution)/shard_map/reduce_scatter | solution.py:268
  617.6 296.1 %reduce-scatter.48.cloned.1.call-start = ((), (), s32[]{:S(2)}) async-start(), calls=%async_computation.34 | async-start | bytes 7077888
  630.3 307.4 %reduce-scatter.28.cloned.1.call-start = ((), (), s32[]{:S(2)}) async-start(), calls=%async_computation.23 | async-start | bytes 1769472 | tf_op jit(solution)/shard_map/reduce_scatter | solution.py:259
  744.5 251.9 %reduce-scatter.40.cloned.1.call-start = ((), (), s32[]{:S(2)}) async-start(), calls=%async_computation.30 | async-start | bytes 626688
  767.3 286.3 %reduce-scatter.32.cloned.1.call-start = ((), (), s32[]{:S(2)}) async-start(), calls=%async_computation.25 | async-start | bytes 626688 | tf_op jit(solution)/shard_map/reduce_scatter | solution.py:285
  791.3 328.5 %reduce-scatter.36.cloned.1.call-start = ((), (), s32[]{:S(2)}) async-start(), calls=%async_computation.27 | async-start | bytes 2506752 | tf_op jit(solution)/shard_map/reduce_scatter | solution.py:288
  851.5 334.1 %reduce-scatter.38.cloned.1.call-start = ((), (), s32[]{:S(2)}) async-start(), calls=%async_computation.28 | async-start | bytes 2506752 | tf_op jit(solution)/shard_map/reduce_scatter | solution.py:291
  918.1 290.4 %reduce-scatter.30.cloned.1.call-start = ((), (), s32[]{:S(2)}) async-start(), calls=%async_computation.24 | async-start | bytes 1769472 | tf_op jit(solution)/shard_map/reduce_scatter | solution.py:262
  919.8 347.3 %reduce-scatter.42.cloned.1.call-start = ((), (), s32[]{:S(2)}) async-start(), calls=%async_computation.31 | async-start | bytes 626688
  939.8 385.1 %reduce-scatter.44.cloned.1.call-start = ((), (), s32[]{:S(2)}) async-start(), calls=%async_computation.32 | async-start | bytes 626688
  943.5 267.3 %copy-start.14 = (f32[768]{0:T(1024)S(1)}, f32[768]{0:T(1024)}, u32[]{:S(2)}) copy-start(f32[768]{0:T(1024)} %get-tuple-element.457) | copy-start | bytes 9220
  943.5 267.3 %copy-start.15 = (f32[768]{0:T(1024)S(1)}, f32[768]{0:T(1024)}, u32[]{:S(2)}) copy-start(f32[768]{0:T(1024)} %get-tuple-element.505) | copy-start | bytes 9220
  943.5 267.3 %copy-start.16 = (f32[768]{0:T(1024)S(1)}, f32[768]{0:T(1024)}, u32[]{:S(2)}) copy-start(f32[768]{0:T(1024)} %get-tuple-element.509) | copy-start | bytes 9220
  943.6 267.3 %copy-start.18 = (f32[3072]{0:T(1024)S(1)}, f32[3072]{0:T(1024)}, u32[]{:S(2)}) copy-start(f32[3072]{0:T(1024)} %get-tuple-element.507) | copy-start | bytes 36868
  943.6 267.3 %copy-start.20 = (f32[768]{0:T(1024)S(1)}, f32[768]{0:T(1024)}, u32[]{:S(2)}) copy-start(f32[768]{0:T(1024)} %get-tuple-element.446) | copy-start | bytes 9220
  943.6 267.3 %copy-start.21 = (f32[768]{0:T(1024)S(1)}, f32[768]{0:T(1024)}, u32[]{:S(2)}) copy-start(f32[768]{0:T(1024)} %get-tuple-element.451) | copy-start | bytes 9220
  943.6 314.9 %copy-start.2 = (bf16[768,768]{1,0:T(8,128)(2,1)S(1)}, bf16[768,768]{1,0:T(8,128)(2,1)}, u32[]{:S(2)}) copy-start(bf16[768,768]{1,0:T(8,128)(2,1)} %all-gather.13.cloned.1.call-done) | copy-start | bytes 3538948
  946.4 312.0 %copy-start.7 = (f32[256,768]{1,0:T(8,128)S(1)}, f32[256,768]{1,0:T(8,128)}, u32[]{:S(2)}) copy-start(f32[256,768]{1,0:T(8,128)} %convolution_add_fusion.3) | copy-start | bytes 2359300
  1251.4 7.6 copy-start.12
  (11 other events, 25.3 us)
Sparse Core Ops, SparseCore 0:
  34.1 20.0 all-gather.12
  55.8 22.7 all-gather.14
  80.9 42.4 all-gather.18
  124.7 21.5 all-gather.10
  148.5 42.5 all-gather.22
  193.2 99.5 all-gather.26
  294.3 20.9 all-gather.16
  316.8 62.6 all-gather.20
  381.1 62.6 all-gather.24
  607.2 134.7 reduce-scatter.23
  744.2 20.8 reduce-scatter.25
  767.4 21.7 reduce-scatter.45
  791.4 59.9 reduce-scatter.33
  853.7 59.9 reduce-scatter.47
  915.9 21.7 reduce-scatter.27
  941.5 54.8 reduce-scatter.39
  999.8 53.8 reduce-scatter.31
  1057.7 62.0 reduce-scatter.35
  1123.6 61.9 reduce-scatter.37
  1187.7 20.7 reduce-scatter.29
  1212.1 54.9 reduce-scatter.41
  1271.0 53.8 reduce-scatter.43
where the time goes:
time: 1340 us; the launch traced here: 1330 us
  waiting for transfers between devices  798 us (60%)
  matrix products  232 us (17%)
  blocking collectives  189 us (14%)
  other arithmetic  51.6 us (4%)
  local copies, waits for them, and re-layouts  43.3 us (3%)
  between operations  17.8 us (1%)
    unnamed x27, waiting for transfers between devices  199 us
    reduce_scatter x1, waiting for transfers between devices, body(): lax.psum_scatter(grad_pair.astype(jnp.bfloat16), 'ctx', scatter_dimension...  112 us
    all_gather x1, waiting for transfers between devices, body(): pair_all = lax.all_gather(pair_local, 'ctx', axis=1, tiled=True)  101 us
    reduce_scatter x1, waiting for transfers between devices, body(): lax.psum_scatter(narrow[4].astype(jnp.bfloat16), 'ctx', scatter_dimension...  64.8 us
    reduce_scatter x1, waiting for transfers between devices, body(): lax.psum_scatter(narrow[5].astype(jnp.bfloat16), 'ctx', scatter_dimension...  64.1 us
    reduce_scatter x1, waiting for transfers between devices, body(): lax.psum_scatter(grad_in_full.astype(jnp.bfloat16), 'fsdp', scatter_dimen...  60.1 us
    dot_general x24, matrix products, head_scores(): jnp.einsum('sqd,skd->sqk', query_head, key_head, preferred_element_type=j...  59.8 us
    unnamed x1, blocking collectives  58.1 us
  transfers between devices with their start and end apart: 22, of which 17 were waited for; matrix products, arithmetic and copies ran while one was open for 12% of the time, Pallas kernels for 0%

commit v1 on v0

--- a/solution.py
+++ b/solution.py
@@ -9,6 +9,18 @@
 masked_score = -1000000000.0
 rows_contract = (((0,), (0,)), ((), ()))
 columns_contract = (((1,), (1,)), ((), ()))
+
+
+def doubled_up(x, axis, dim):
+    ways, here = (lax.axis_size(axis), lax.axis_index(axis))
+    grown, reach = (x, 1)
+    while reach < ways:
+        theirs = lax.ppermute(grown, axis, [(d, d ^ reach) for d in range(ways)])
+        mine_first = jnp.concatenate([grown, theirs], axis=dim)
+        theirs_first = jnp.concatenate([theirs, grown], axis=dim)
+        grown = jnp.where(here & reach == 0, mine_first, theirs_first)
+        reach = 2 * reach
+    return grown
 
 
 def layer_norm(stream, gain_vec, shift_vec):
@@ -167,7 +179,7 @@
         lax.all_gather(row_parts[2], "fsdp", axis=1, tiled=True),
         lax.all_gather(row_parts[3], "fsdp", axis=1, tiled=True),
         lax.all_gather(row_parts[4], "fsdp", axis=1, tiled=True),
-        lax.all_gather(row_parts[5], "fsdp", axis=1, tiled=True),
+        doubled_up(row_parts[5], "fsdp", 1),
     )
     query_full, key_full, value_full, out_full, in_full, down_full = full_mats
     query_vec = row_parts[6].astype(jnp.float32)

time: 1340 us -> 1290 us (0.963)
  waiting for transfers between devices: 798 us -> 744 us
    all_gather x1 -> x0, waiting for transfers between devices: 52.1 us -> none  [body(): lax.all_gather(row_parts[5], 'fsdp', axis=1, tiled=True)]
    all_gather x1, waiting for transfers between devices: 21.9 us -> 0.02 us  [body(): lax.all_gather(down_weight, 'ctx', axis=0, tiled=True)]
    all_gather x1, waiting for transfers between devices: 0.02 us -> 21.1 us  [body(): lax.all_gather(in_weight, 'ctx', axis=0, tiled=True)]
    unnamed x27 -> x26, waiting for transfers between devices: 199 us -> 199 us
    unnamed x106 -> x104, local copies, waits for them, and re-layouts: 31.1 us -> 30.8 us
  transfers between devices with their start and end apart: 22 -> 22, of which waited for: 17 -> 16; matrix products, arithmetic and copies ran while one was open for 12% -> 12% of each run, Pallas kernels for 0% -> 0%
where the time goes in v1:
time: 1290 us; the launch traced here: 1280 us
  waiting for transfers between devices  744 us (58%)
  matrix products  233 us (18%)
  blocking collectives  189 us (15%)
  other arithmetic  51.6 us (4%)
  local copies, waits for them, and re-layouts  43 us (3%)
  between operations  17.9 us (1%)
    unnamed x26, waiting for transfers between devices  199 us
    reduce_scatter x1, waiting for transfers between devices, body(): lax.psum_scatter(grad_pair.astype(jnp.bfloat16), 'ctx', scatter_dimension...  112 us
    all_gather x1, waiting for transfers between devices, body(): pair_all = lax.all_gather(pair_local, 'ctx', axis=1, tiled=True)  102 us
    reduce_scatter x1, waiting for transfers between devices, body(): lax.psum_scatter(narrow[4].astype(jnp.bfloat16), 'ctx', scatter_dimension...  64.7 us
    reduce_scatter x1, waiting for transfers between devices, body(): lax.psum_scatter(narrow[5].astype(jnp.bfloat16), 'ctx', scatter_dimension...  64 us
    reduce_scatter x1, waiting for transfers between devices, body(): lax.psum_scatter(grad_in_full.astype(jnp.bfloat16), 'fsdp', scatter_dimen...  60 us
    dot_general x24, matrix products, head_scores(): jnp.einsum('sqd,skd->sqk', query_head, key_head, preferred_element_type=j...  59.8 us
    unnamed x1, blocking collectives  58 us
  transfers between devices with their start and end apart: 22, of which 16 were waited for; matrix products, arithmetic and copies ran while one was open for 12% of the time, Pallas kernels for 0%

profile of v1, /device:TPU:0, one launch (start us, length us, event | category | flops | bytes accessed | tf_op | source)
XLA Modules:
  0.0 1282.2 jit_solution(10702796396701222458)
XLA Ops:
  7.4 26.6 %all_gather.66 = bf16[768,384]{1,0:T(8,128)(2,1)} all-gather(bf16[48,384]{1,0:T(8,128)(2,1)} %param.26), channel_id=1, replica_groups=mesh['ctx'=16,'fsdp'=2] {'ctx'}, dimensions={0}, use_global_device_ids=true | all-gather | bytes 626688 | tf_op jit(solution)/shard_map/all_gather | solution.py:161
  34.1 20.7 %all_gather.68 = bf16[768,384]{1,0:T(8,128)(2,1)} all-gather(bf16[48,384]{1,0:T(8,128)(2,1)} %param.27), channel_id=1, replica_groups=mesh['ctx'=16,'fsdp'=2] {'ctx'}, dimensions={0}, use_global_device_ids=true | all-gather | bytes 626688 | tf_op jit(solution)/shard_map/all_gather | solution.py:162
  54.8 22.2 %all_gather.63 = bf16[768,384]{1,0:T(8,128)(2,1)} all-gather(bf16[48,384]{1,0:T(8,128)(2,1)} %param.25), channel_id=1, replica_groups=mesh['ctx'=16,'fsdp'=2] {'ctx'}, dimensions={0}, use_global_device_ids=true | all-gather | bytes 626688 | tf_op jit(solution)/shard_map/all_gather | solution.py:160
  82.4 58.0 %all-reduce.10 = (bf16[768]{0:T(1024)(128)(2,1)S(1)}, bf16[768]{0:T(1024)(128)(2,1)S(1)}, bf16[3072]{0:T(1024)(128)(2,1)S(1)}, bf16[768]{0:T(1024)(128)(2,1)S(1)...) all-reduce(bf16[768]{0:T(1024)(128)(2,1)S(1)} %dynamic-update-slice, ...), channel_id=1, replica_groups=mesh['ctx'=16,'fsdp'=2] {'ctx'}, use_global_device_ids=true, to_apply=%add | all-reduce | flops 9216 | bytes 36864
  144.9 20.7 %all_gather.72 = bf16[768,384]{1,0:T(8,128)(2,1)} all-gather(bf16[48,384]{1,0:T(8,128)(2,1)S(1)} %copy-done.14), channel_id=1, replica_groups=mesh['ctx'=16,'fsdp'=2] {'ctx'}, dimensions={0}, use_global_device_ids=true | all-gather | bytes 626688 | tf_op jit(solution)/shard_map/all_gather | solution.py:163
  169.8 21.1 %all-gather.18.cloned.1.call-done = bf16[768,1536]{1,0:T(8,128)(2,1)} async-done(((bf16[48,1536]{1,0:T(8,128)(2,1)}), bf16[768,1536]{1,0:T(8,128)(2,1)}) %all-gather.18.cloned.1.call-update) | async-done | bytes 2359312 | tf_op jit(solution)/shard_map/all_gather | solution.py:164
  191.0 101.6 %all-gather.24.cloned.1.call-done = bf16[4096,1536]{1,0:T(8,128)(2,1)} async-done(((bf16[256,1536]{1,0:T(8,128)(2,1)}), bf16[4096,1536]{1,0:T(8,128)(2,1)}) %all-gather.24.cloned.1.call-update) | async-done | bytes 12582928 | tf_op jit(solution)/shard_map/all_gather | solution.py:206
  292.6 77.9 %while.36 = (s32[]{:T(128)}, bf16[1,256,768]{1,2,0:T(8,128)(2,1)S(1)}, f32[12,1,256]{2,1,0:T(1,128)S(1)}, bf16[1,256,768]{2,1,0:T(8,128)(2,1)S(1)}, bf16[1,4096,...) while((s32[]{:T(128)}, ...), condition=%wide.region_3.4_spmd.clone, body=%wide.region_0.3_spmd.clone.sunk | while | flops 276827904 | bytes 14829822 | solution.py:86
  316.1 2.7 fusion.148
  322.5 2.9 fusion.148
  329.2 2.8 fusion.148
  372.8 6.6 all-gather.20.cloned.1.call-done
  379.4 9.9 multiply_convert_fusion.1
  389.3 4.6 fusion.104
  397.4 6.1 convert_reduce_fusion
  407.8 6.1 broadcast_in_dim.102
  413.8 142.1 %while.37 = (s32[]{:T(128)}, bf16[1,256,768]{1,2,0:T(8,128)(2,1)S(1)}, bf16[1,4096,1536]{1,2,0:T(8,128)(2,1)}, bf16[1,256,768]{2,1,0:T(8,128)(2,1)S(1)}, bf16[1,...) while((s32[]{:T(128)}, ...), condition=%wide.region_14.15_spmd.clone, body=%wide.region_12.14_spmd.clone.sunk | while | flops 680808192 | bytes 37041444 | solution.py:128
  416.5 2.8 multiply_reduce_fusion.6
  428.4 2.7 multiply_reduce_fusion.6
  440.3 2.8 multiply_reduce_fusion.6
  452.1 2.7 multiply_reduce_fusion.6
  463.9 2.7 multiply_reduce_fusion.6
  475.7 2.7 multiply_reduce_fusion.6
  487.6 2.7 multiply_reduce_fusion.6
  499.4 2.7 multiply_reduce_fusion.6
  511.3 2.8 multiply_reduce_fusion.6
  523.1 2.8 multiply_reduce_fusion.6
  534.9 2.8 multiply_reduce_fusion.6
  546.8 2.8 multiply_reduce_fusion.6
  560.7 5.7 convolution_convert_fusion.1
  568.2 3.7 convolution_convert_fusion
  571.9 7.1 copy.50
  579.1 111.7 %reduce-scatter.24.cloned.1.call-done = bf16[1,256,1536]{1,2,0:T(8,128)(2,1)} async-done(((bf16[1,4096,1536]{1,2,0:T(8,128)(2,1)}), bf16[1,256,1536]{1,2,0:T(8,128)(2,1)}) %reduce-scatter.24.cloned.1.call-update) | async-done | bytes 786448 | tf_op jit(solution)/shard_map/reduce_scatter | solution.py:242
  693.4 20.4 %reduce-scatter.26.cloned.1.call-done = bf16[768,384]{0,1:T(8,128)(2,1)} async-done(((bf16[768,768]{0,1:T(8,128)(2,1)}), bf16[768,384]{0,1:T(8,128)(2,1)}) %reduce-scatter.26.cloned.1.call-update) | async-done | bytes 589840 | tf_op jit(solution)/shard_map/reduce_scatter | solution.py:268
  716.1 21.9 %reduce-scatter.46.cloned.1.call-done = bf16[384,768]{1,0:T(8,128)(2,1)} async-done(((bf16[768,768]{1,0:T(8,128)(2,1)}), bf16[384,768]{1,0:T(8,128)(2,1)}) %reduce-scatter.46.cloned.1.call-update) | async-done | bytes 589840
  740.2 60.0 %reduce-scatter.34.cloned.1.call-done = bf16[768,1536]{1,0:T(8,128)(2,1)} async-done(((bf16[768,3072]{1,0:T(8,128)(2,1)}), bf16[768,1536]{1,0:T(8,128)(2,1)}) %reduce-scatter.34.cloned.1.call-update) | async-done | bytes 2359312 | tf_op jit(solution)/shard_map/reduce_scatter | solution.py:280
  800.2 62.4 %reduce-scatter.48.cloned.1.call-done = bf16[384,3072]{1,0:T(8,128)(2,1)} async-done(((bf16[768,3072]{1,0:T(8,128)(2,1)}), bf16[384,3072]{1,0:T(8,128)(2,1)}) %reduce-scatter.48.cloned.1.call-update) | async-done | bytes 2359312
  862.6 4.4 copy.51
  868.6 17.9 %reduce-scatter.28.cloned.1.call-done = bf16[768,384]{0,1:T(8,128)(2,1)} async-done(((bf16[768,768]{0,1:T(8,128)(2,1)}), bf16[768,384]{0,1:T(8,128)(2,1)}) %reduce-scatter.28.cloned.1.call-update) | async-done | bytes 589840 | tf_op jit(solution)/shard_map/reduce_scatter | solution.py:271
  892.2 2.8 convolution_add_fusion.3
  895.0 50.1 %reduce-scatter.40.cloned.1.call-done = bf16[48,384]{1,0:T(8,128)(2,1)} async-done(((bf16[768,384]{1,0:T(8,128)(2,1)}), bf16[48,384]{1,0:T(8,128)(2,1)}) %reduce-scatter.40.cloned.1.call-update) | async-done | bytes 36880
  946.7 55.7 %reduce-scatter.32.cloned.1.call-done = bf16[48,384]{1,0:T(8,128)(2,1)} async-done(((bf16[768,384]{1,0:T(8,128)(2,1)}), bf16[48,384]{1,0:T(8,128)(2,1)}) %reduce-scatter.32.cloned.1.call-update) | async-done | bytes 36880 | tf_op jit(solution)/shard_map/reduce_scatter | solution.py:297
  1003.8 64.7 %reduce-scatter.36.cloned.1.call-done = bf16[48,1536]{1,0:T(8,128)(2,1)} async-done(((bf16[768,1536]{1,0:T(8,128)(2,1)}), bf16[48,1536]{1,0:T(8,128)(2,1)}) %reduce-scatter.36.cloned.1.call-update) | async-done | bytes 147472 | tf_op jit(solution)/shard_map/reduce_scatter | solution.py:300
  1070.2 64.0 %reduce-scatter.38.cloned.1.call-done = bf16[192,384]{1,0:T(8,128)(2,1)} async-done(((bf16[3072,384]{1,0:T(8,128)(2,1)}), bf16[192,384]{1,0:T(8,128)(2,1)}) %reduce-scatter.38.cloned.1.call-update) | async-done | bytes 147472 | tf_op jit(solution)/shard_map/reduce_scatter | solution.py:303
  1135.9 21.5 %reduce-scatter.30.cloned.1.call-done = bf16[768,384]{0,1:T(8,128)(2,1)} async-done(((bf16[768,768]{0,1:T(8,128)(2,1)}), bf16[768,384]{0,1:T(8,128)(2,1)}) %reduce-scatter.30.cloned.1.call-update) | async-done | bytes 589840 | tf_op jit(solution)/shard_map/reduce_scatter | solution.py:274
  1159.7 40.3 %all-reduce.9 = (f32[768]{0:T(1024)S(1)}, f32[768]{0:T(1024)S(1)}, f32[768]{0:T(1024)S(1)}, f32[768]{0:T(1024)S(1)}, f32[768]{0:T(1024)S(1)}, /*index=5*/f32[307...) all-reduce(f32[768]{0:T(1024)S(1)} %convert_reduce_fusion.4, ...), channel_id=1, replica_groups=mesh['ctx'=16,'fsdp'=2] {'ctx','fsdp'}, use_global_device_ids=true, to_apply=%region_29.30 | all-reduce | flops 9220 | bytes 73760 | tf_op jit(solution)/shard_map/psum | solution.py:315
  1209.0 6.7 reduce-scatter.42.cloned.1.call-done
  1217.3 56.3 %reduce-scatter.44.cloned.1.call-done = bf16[48,384]{1,0:T(8,128)(2,1)} async-done(((bf16[768,384]{1,0:T(8,128)(2,1)}), bf16[48,384]{1,0:T(8,128)(2,1)}) %reduce-scatter.44.cloned.1.call-update) | async-done | bytes 36880
  (364 shorter events, 240.2 us)
Async XLA Ops:
  7.2 71.1 %copy-start.33 = (u32[32]{0:T(128)S(1)}, u32[32]{0:T(128)}, u32[]{:S(2)}) copy-start(u32[32]{0:T(128)} %constant.311) | copy-start | bytes 388
  7.2 73.0 %copy-start.24 = (bf16[48]{0:T(256)(128)(2,1)S(1)}, bf16[48]{0:T(256)(128)(2,1)}, u32[]{:S(2)}) copy-start(bf16[48]{0:T(256)(128)(2,1)} %param.38) | copy-start | bytes 292
  7.2 73.2 %copy-start.25 = (bf16[48]{0:T(256)(128)(2,1)S(1)}, bf16[48]{0:T(256)(128)(2,1)}, u32[]{:S(2)}) copy-start(bf16[48]{0:T(256)(128)(2,1)} %param.37) | copy-start | bytes 292
  7.2 73.5 %copy-start.26 = (bf16[48]{0:T(256)(128)(2,1)S(1)}, bf16[48]{0:T(256)(128)(2,1)}, u32[]{:S(2)}) copy-start(bf16[48]{0:T(256)(128)(2,1)} %param.34) | copy-start | bytes 292
  7.2 73.7 %copy-start.27 = (bf16[48]{0:T(256)(128)(2,1)S(1)}, bf16[48]{0:T(256)(128)(2,1)}, u32[]{:S(2)}) copy-start(bf16[48]{0:T(256)(128)(2,1)} %param.35) | copy-start | bytes 292
  7.2 73.9 %copy-start.28 = (bf16[48]{0:T(256)(128)(2,1)S(1)}, bf16[48]{0:T(256)(128)(2,1)}, u32[]{:S(2)}) copy-start(bf16[48]{0:T(256)(128)(2,1)} %param.33) | copy-start | bytes 292
  7.3 74.1 %copy-start.29 = (bf16[48]{0:T(256)(128)(2,1)S(1)}, bf16[48]{0:T(256)(128)(2,1)}, u32[]{:S(2)}) copy-start(bf16[48]{0:T(256)(128)(2,1)} %param.32) | copy-start | bytes 292
  7.3 74.4 %copy-start.30 = (bf16[48]{0:T(256)(128)(2,1)S(1)}, bf16[48]{0:T(256)(128)(2,1)}, u32[]{:S(2)}) copy-start(bf16[48]{0:T(256)(128)(2,1)} %param.31) | copy-start | bytes 292
  7.3 74.6 %copy-start.31 = (bf16[48]{0:T(256)(128)(2,1)S(1)}, bf16[48]{0:T(256)(128)(2,1)}, u32[]{:S(2)}) copy-start(bf16[48]{0:T(256)(128)(2,1)} %param.39) | copy-start | bytes 292
  7.3 74.8 %copy-start.32 = (bf16[192]{0:T(256)(128)(2,1)S(1)}, bf16[192]{0:T(256)(128)(2,1)}, u32[]{:S(2)}) copy-start(bf16[192]{0:T(256)(128)(2,1)} %param.36) | copy-start | bytes 1156
  7.3 133.1 %copy-start = (bf16[1,256,768]{2,1,0:T(8,128)(2,1)S(1)}, bf16[1,256,768]{2,1,0:T(8,128)(2,1)}, u32[]{:S(2)}) copy-start(bf16[1,256,768]{2,1,0:T(8,128)(2,1)} %param.22) | copy-start | bytes 1179652
  7.3 133.1 %all-gather.12.cloned.1.call-start = ((), (), s32[]{:S(2)}) async-start(), calls=%async_computation.14 | async-start | bytes 1769472 | tf_op jit(solution)/shard_map/all_gather | solution.py:178
  34.0 108.1 %all-gather.14.cloned.1.call-start = ((), (), s32[]{:S(2)}) async-start(), calls=%async_computation.15 | async-start | bytes 1769472 | tf_op jit(solution)/shard_map/all_gather | solution.py:179
  54.8 111.7 %all-gather.10.cloned.1.call-start = ((), (), s32[]{:S(2)}) async-start(), calls=%async_computation.13 | async-start | bytes 1769472 | tf_op jit(solution)/shard_map/all_gather | solution.py:177
  77.1 91.1 %all-gather.22.cloned.1.call-start = ((), (), s32[]{:S(2)}) async-start(), calls=%async_computation.19 | async-start | bytes 2506752 | tf_op jit(solution)/shard_map/all_gather | solution.py:165
  77.7 113.2 %all-gather.18.cloned.1.call-start = ((), (), s32[]{:S(2)}) async-start(), calls=%async_computation.17 | async-start | bytes 2506752 | tf_op jit(solution)/shard_map/all_gather | solution.py:164
  78.3 214.3 %all-gather.24.cloned.1.call-start = ((), (), s32[]{:S(2)}) async-start(), calls=%async_computation.28 | async-start | bytes 13369344 | tf_op jit(solution)/shard_map/all_gather | solution.py:206
  144.9 225.7 %all-gather.16.cloned.1.call-start = ((), (), s32[]{:S(2)}) async-start(), calls=%async_computation.16 | async-start | bytes 1769472 | tf_op jit(solution)/shard_map/all_gather | solution.py:180
  165.6 213.8 %all-gather.20.cloned.1.call-start = ((), (), s32[]{:S(2)}) async-start(), calls=%async_computation.18 | async-start | bytes 7077888 | tf_op jit(solution)/shard_map/all_gather | solution.py:181
  168.2 221.0 %collective-permute-start = (bf16[3072,384]{1,0:T(8,128)(2,1)}, bf16[3072,384]{1,0:T(8,128)(2,1)}, u32[]{:S(2)}, u32[]{:S(2)}) collective-permute-start(bf16[3072,384]{1,0:T(8,128)(2,1)} %all-gather.22.cloned.1.call-done), channel_id=1, source_target_pairs={{0,1},{1,0},{2,3},{3,2},{4,5},{5,4},{6,7},{7,6},{8,9},{9,8},{10,11... | collective-permute-start | bytes 7077896 | tf_op jit(solution)/shard_map/ppermute | solution.py:18
  190.9 499.9 %reduce-scatter.24.cloned.1.call-start = ((), (), s32[]{:S(2)}) async-start(), calls=%async_computation.20 | async-start | bytes 13369344 | tf_op jit(solution)/shard_map/reduce_scatter | solution.py:242
  370.5 18.7 %copy-start.4 = (bf16[1,256,768]{1,2,0:T(8,128)(2,1)}, bf16[1,256,768]{1,2,0:T(8,128)(2,1)S(1)}, u32[]{:S(2)}) copy-start(bf16[1,256,768]{1,2,0:T(8,128)(2,1)S(1)} %get-tuple-element.372) | copy-start | bytes 1179652
  372.8 33.1 %copy-start.18 = (f32[256]{0:T(256)}, f32[256]{0:T(256)S(1)}, u32[]{:S(2)}) copy-start(f32[256]{0:T(256)S(1)} %fusion.91) | copy-start | bytes 3076
  379.4 9.9 copy-start.23
  395.5 8.1 slice-start
  397.4 6.1 copy-start.9
  397.4 6.2 slice-start.1
  555.9 157.9 %reduce-scatter.26.cloned.1.call-start = ((), (), s32[]{:S(2)}) async-start(), calls=%async_computation.21 | async-start | bytes 1769472 | tf_op jit(solution)/shard_map/reduce_scatter | solution.py:268
  557.5 180.5 %reduce-scatter.46.cloned.1.call-start = ((), (), s32[]{:S(2)}) async-start(), calls=%async_computation.32 | async-start | bytes 1769472
  560.6 239.5 %reduce-scatter.34.cloned.1.call-start = ((), (), s32[]{:S(2)}) async-start(), calls=%async_computation.25 | async-start | bytes 7077888 | tf_op jit(solution)/shard_map/reduce_scatter | solution.py:280
  566.4 296.2 %reduce-scatter.48.cloned.1.call-start = ((), (), s32[]{:S(2)}) async-start(), calls=%async_computation.33 | async-start | bytes 7077888
  579.0 307.4 %reduce-scatter.28.cloned.1.call-start = ((), (), s32[]{:S(2)}) async-start(), calls=%async_computation.22 | async-start | bytes 1769472 | tf_op jit(solution)/shard_map/reduce_scatter | solution.py:271
  693.3 251.8 %reduce-scatter.40.cloned.1.call-start = ((), (), s32[]{:S(2)}) async-start(), calls=%async_computation.29 | async-start | bytes 626688
  716.0 286.4 %reduce-scatter.32.cloned.1.call-start = ((), (), s32[]{:S(2)}) async-start(), calls=%async_computation.24 | async-start | bytes 626688 | tf_op jit(solution)/shard_map/reduce_scatter | solution.py:297
  740.1 328.4 %reduce-scatter.36.cloned.1.call-start = ((), (), s32[]{:S(2)}) async-start(), calls=%async_computation.26 | async-start | bytes 2506752 | tf_op jit(solution)/shard_map/reduce_scatter | solution.py:300
  800.2 334.1 %reduce-scatter.38.cloned.1.call-start = ((), (), s32[]{:S(2)}) async-start(), calls=%async_computation.27 | async-start | bytes 2506752 | tf_op jit(solution)/shard_map/reduce_scatter | solution.py:303
  867.0 290.4 %reduce-scatter.30.cloned.1.call-start = ((), (), s32[]{:S(2)}) async-start(), calls=%async_computation.23 | async-start | bytes 1769472 | tf_op jit(solution)/shard_map/reduce_scatter | solution.py:274
  868.6 347.1 %reduce-scatter.42.cloned.1.call-start = ((), (), s32[]{:S(2)}) async-start(), calls=%async_computation.30 | async-start | bytes 626688
  888.6 385.0 %reduce-scatter.44.cloned.1.call-start = ((), (), s32[]{:S(2)}) async-start(), calls=%async_computation.31 | async-start | bytes 626688
  892.1 267.6 %copy-start.15 = (f32[768]{0:T(1024)S(1)}, f32[768]{0:T(1024)}, u32[]{:S(2)}) copy-start(f32[768]{0:T(1024)} %get-tuple-element.457) | copy-start | bytes 9220
  892.1 267.6 %copy-start.16 = (f32[768]{0:T(1024)S(1)}, f32[768]{0:T(1024)}, u32[]{:S(2)}) copy-start(f32[768]{0:T(1024)} %get-tuple-element.505) | copy-start | bytes 9220
  892.1 267.6 %copy-start.17 = (f32[768]{0:T(1024)S(1)}, f32[768]{0:T(1024)}, u32[]{:S(2)}) copy-start(f32[768]{0:T(1024)} %get-tuple-element.507) | copy-start | bytes 9220
  892.1 267.6 %copy-start.19 = (f32[3072]{0:T(1024)S(1)}, f32[3072]{0:T(1024)}, u32[]{:S(2)}) copy-start(f32[3072]{0:T(1024)} %get-tuple-element.528) | copy-start | bytes 36868
  892.2 267.6 %copy-start.21 = (f32[768]{0:T(1024)S(1)}, f32[768]{0:T(1024)}, u32[]{:S(2)}) copy-start(f32[768]{0:T(1024)} %get-tuple-element.446) | copy-start | bytes 9220
  892.2 267.6 %copy-start.22 = (f32[768]{0:T(1024)S(1)}, f32[768]{0:T(1024)}, u32[]{:S(2)}) copy-start(f32[768]{0:T(1024)} %get-tuple-element.451) | copy-start | bytes 9220
  892.2 315.0 %copy-start.2 = (bf16[768,768]{1,0:T(8,128)(2,1)S(1)}, bf16[768,768]{1,0:T(8,128)(2,1)}, u32[]{:S(2)}) copy-start(bf16[768,768]{1,0:T(8,128)(2,1)} %all-gather.12.cloned.1.call-done) | copy-start | bytes 3538948
  895.0 312.2 %copy-start.8 = (f32[256,768]{1,0:T(8,128)S(1)}, f32[256,768]{1,0:T(8,128)}, u32[]{:S(2)}) copy-start(f32[256,768]{1,0:T(8,128)} %convolution_add_fusion.3) | copy-start | bytes 2359300
  1200.1 7.6 copy-start.13
  (10 other events, 27.0 us)
Sparse Core Ops, SparseCore 0:
  34.1 20.0 all-gather.11
  55.8 22.7 all-gather.13
  80.1 22.7 all-gather.9
  105.1 42.6 all-gather.21
  149.9 40.9 all-gather.17
  193.0 99.5 all-gather.23
  294.1 20.9 all-gather.15
  316.7 62.6 all-gather.19
  556.0 134.7 reduce-scatter.23
  692.9 20.8 reduce-scatter.25
  716.2 21.7 reduce-scatter.45
  740.1 59.9 reduce-scatter.33
  802.5 59.9 reduce-scatter.47
  864.7 21.7 reduce-scatter.27
  890.3 54.7 reduce-scatter.39
  948.5 53.8 reduce-scatter.31
  1006.5 61.9 reduce-scatter.35
  1072.2 62.0 reduce-scatter.37
  1136.6 20.7 reduce-scatter.29
  1160.8 54.8 reduce-scatter.41
  1219.7 53.8 reduce-scatter.43
